TPU v7x, 32 devices: a whole 2x2x4 slice. The times are simulated.
32 devices in a mesh: user: 8 (over z, y), item: 4 (over x, core).
Axes of the slice: x: 2, y: 2, z: 4, core: 2. Of those that a mesh axis runs over, the one named last changes fastest.
Arguments:
- v_start: bfloat16 [32768, 64], P(('user', 'item')), may hold values from -6 to 6
- locked: bfloat16 [32768, 32], P(('user', 'item')), may hold values from -0.0625 to 0.0625
- tile_rows: int32 [32, 512], P(('user', 'item')), may hold values from 0 to 63, as said below
- tile_cols: int32 [32, 512], P(('user', 'item')), may hold values from 0 to 63
- tile_seeds: int32 [32, 512], P(('user', 'item')), may hold values from 0 to 1048575
- tile_count: int32 [32, 1], P(('user', 'item')), may hold values from 128 to 512, as said below
Outputs:
- u_factor: bfloat16 [65536, 64], P(('user', 'item'))
- v_next: float32 [32768, 64], P(('user', 'item'))
Inputs may be any that keep to these rules, and one draw needn't show every extreme that they name: `tile_count`: at most 512 live slots a device, and one device holds exactly 512. `tile_rows`: A device's slots name distinct (row, column) pairs.
All inputs are finite; a program needn't handle non-finite values.
Results may differ from a plain program's by a relative error of at most 0.0049.
Values may be sent and summed in bfloat16 or wider, within the bound.
A program may use at most 64 MiB of HBM per device.

v0:
```python
import jax
import jax.numpy as jnp
from jax import lax
from jax.sharding import PartitionSpec as P

TILE = 128
RB = 64


tile_batch = 16


def tile_values(seeds, tile):
    rowpos = lax.broadcasted_iota(jnp.int32, (tile, tile), 0)
    colpos = lax.broadcasted_iota(jnp.int32, (tile, tile), 1)
    hashed = (rowpos * tile + colpos)[None, :, :] * 40503 + seeds[:, None, None] * 9973
    hashed = jnp.bitwise_xor(hashed, jnp.right_shift(hashed, 13))
    hashed = hashed * 1597334677
    hashed = jnp.bitwise_xor(hashed, jnp.right_shift(hashed, 16))
    levels = jnp.bitwise_and(jnp.right_shift(hashed, 8), 255) - 128
    return (levels.astype(jnp.float32) * (1.0 / 1024.0)).astype(jnp.bfloat16)


def start_reduce(proj):
    proj = lax.psum(proj, ("user", "item"))
    return (proj, proj)


def on_device(v_start, locked, tile_rows, tile_cols, tile_seeds, tile_count):
    high = lax.Precision.HIGHEST
    tile = TILE
    width = v_start.shape[1]
    rows = tile_rows[0]
    cols = tile_cols[0]
    seeds = tile_seeds[0]
    count = tile_count[0, 0]
    slots = rows.shape[0]
    proj_local = jnp.dot(locked.T, v_start, preferred_element_type=jnp.float32)
    proj, gram = start_reduce(proj_local)
    deflated = (
        v_start.astype(jnp.float32) - jnp.dot(locked.astype(jnp.float32), proj, precision=high)
    ).astype(jnp.bfloat16)
    vslab = lax.all_gather(deflated, "user", axis=0, tiled=True)
    nblocks = vslab.shape[0] // tile
    vblocks = vslab.reshape(nblocks, tile, width)
    steps = (count + tile_batch - 1) // tile_batch
    offsets = jnp.arange(tile_batch, dtype=jnp.int32)

    def forward_step(g, carry):
        buffer, upart = carry
        start = g * tile_batch
        grows = lax.dynamic_slice_in_dim(rows, start, tile_batch)
        gcols = lax.dynamic_slice_in_dim(cols, start, tile_batch)
        gseeds = lax.dynamic_slice_in_dim(seeds, start, tile_batch)
        tiles = tile_values(gseeds, tile)
        buffer = lax.dynamic_update_slice_in_dim(buffer, tiles, start, 0)
        prod = jnp.einsum("gab,gbk->gak", tiles, vblocks[gcols], preferred_element_type=jnp.float32)
        prod = jnp.where((start + offsets < count)[:, None, None], prod, 0.0)
        return (buffer, upart.at[grows].add(prod))

    buffer, upart = lax.fori_loop(
        0,
        steps,
        forward_step,
        (jnp.zeros((slots, tile, tile), jnp.bfloat16), jnp.zeros((RB, tile, width), jnp.float32)),
    )
    usum = lax.psum(upart.reshape(RB * tile, width), "item")
    uslab = usum.astype(jnp.bfloat16)
    per_dev = RB * tile // lax.axis_size("item")
    u_factor = lax.dynamic_slice_in_dim(uslab, lax.axis_index("item") * per_dev, per_dev, 0)
    ublocks = uslab.reshape(RB, tile, width)

    def backward_step(g, wpart):
        start = g * tile_batch
        grows = lax.dynamic_slice_in_dim(rows, start, tile_batch)
        gcols = lax.dynamic_slice_in_dim(cols, start, tile_batch)
        tiles = lax.dynamic_slice_in_dim(buffer, start, tile_batch, 0)
        prod = jnp.einsum("gab,gak->gbk", tiles, ublocks[grows], preferred_element_type=jnp.float32)
        prod = jnp.where((start + offsets < count)[:, None, None], prod, 0.0)
        return wpart.at[gcols].add(prod)

    wpart = lax.fori_loop(0, steps, backward_step, jnp.zeros((nblocks, tile, width), jnp.float32))
    back = lax.psum_scatter(
        wpart.reshape(nblocks * tile, width), "user", scatter_dimension=0, tiled=True
    )
    lockf = locked.astype(jnp.float32)
    proj_back = jnp.dot(lockf.T, back, precision=high)
    total_items = nblocks * tile * lax.axis_size("item")
    proj2 = lax.psum(proj_back, ("user", "item"))
    rest = back - jnp.dot(lockf, proj2, precision=high)
    colsq = lax.psum(jnp.sum(rest * rest, axis=0), ("user", "item"))
    v_next = rest / jnp.sqrt(colsq / total_items + 1e-06)
    return (u_factor, v_next)


def solution(mesh):
    in_specs = (
        P(("user", "item"), None),
        P(("user", "item"), None),
        P(("user", "item"), None),
        P(("user", "item"), None),
        P(("user", "item"), None),
        P(("user", "item"), None),
    )
    out_specs = (P(("user", "item"), None), P(("user", "item"), None))
    return jax.shard_map(
        on_device, mesh=mesh, in_specs=in_specs, out_specs=out_specs, check_vma=False
    )
```

profile of v0, /device:TPU:0, one launch (start us, length us, event | category | flops | bytes accessed | tf_op | source)
XLA Modules:
  0.0 716.5 jit_solution(3770280152101505471)
XLA Ops:
  9.1 42.0 %psum.28 = f32[32,64]{1,0:T(8,128)S(1)} all-reduce(f32[32,64]{1,0:T(8,128)S(1)} %fusion.27), channel_id=1, replica_groups=mesh['user'=8,'item'=4] {'user','item'}, use_global_device_ids=true, to_apply=%region_0.0 | all-reduce | flops 2048 | bytes 16384 | tf_op jit(solution)/shard_map/psum | solution.py:25
  53.7 39.5 %all-gather.2.cloned.1.call-done = bf16[8192,64]{0,1:T(8,128)(2,1)} async-done(((bf16[1024,64]{0,1:T(8,128)(2,1)}), bf16[8192,64]{0,1:T(8,128)(2,1)}) %all-gather.2.cloned.1.call-update) | async-done | bytes 1048592 | tf_op jit(solution)/shard_map/all_gather | solution.py:43
  93.2 2.8 copy.16
  96.0 6.3 broadcast_in_dim.53
  103.0 78.4 %while.26 = (s32[]{:T(128)}, bf16[512,128,128]{2,1,0:T(8,128)(2,1)}, f32[64,128,64]{1,2,0:T(8,128)S(1)}, s32[]{:T(128)}, s32[512]{0:T(512)}, /*index=5*/s32[512]...) while((s32[]{:T(128)}, ...), condition=%wide.region_3.4_spmd.clone, body=%wide.region_1.3_spmd.clone.sunk | while | flops 40142100 | bytes 3610527 | solution.py:61
  117.3 2.2 gather_fusion
  124.5 2.2 gather_fusion
  138.7 2.2 gather_fusion
  182.9 54.7 %all-reduce.1 = bf16[8192,64]{0,1:T(8,128)(2,1)S(1)} all-reduce(f32[8192,64]{0,1:T(8,128)} %copy_bitcast_fusion.1), channel_id=1, replica_groups=mesh['user'=8,'item'=4] {'item'}, use_global_device_ids=true, to_apply=%region_4.5 | all-reduce | flops 524288 | bytes 3145728 | tf_op jit(solution)/shard_map/psum | solution.py:67
  239.7 63.0 %while.27 = (s32[]{:T(128)}, f32[64,128,64]{1,2,0:T(8,128)S(1)}, s32[]{:T(128)}, s32[512]{0:T(512)S(1)}, s32[]{:T(128)}, /*index=5*/bf16[512,128,128]{2,1,0:T(8,...) while((s32[]{:T(128)}, f32[64,128,64]{1,2,0:T(8,128)S(1)}, ...), condition=%wide.region_7.8_spmd.clone, body=%wide.region_5.7_spmd.clone.sunk | while | flops 33817732 | bytes 3412627 | solution.py:82
  239.8 2.2 gather_fusion.1
  245.6 2.2 gather_fusion.1
  251.3 2.2 gather_fusion.1
  257.0 2.2 gather_fusion.1
  262.7 2.2 gather_fusion.1
  268.5 2.2 gather_fusion.1
  274.2 2.2 gather_fusion.1
  279.9 2.2 gather_fusion.1
  285.6 2.2 gather_fusion.1
  291.4 2.2 gather_fusion.1
  297.1 2.2 gather_fusion.1
  305.9 321.0 %reduce-scatter.2.cloned.1.call-done = f32[1024,64]{0,1:T(8,128)} async-done(((f32[8192,64]{0,1:T(8,128)}), f32[1024,64]{0,1:T(8,128)}) %reduce-scatter.2.cloned.1.call-update) | async-done | bytes 262160 | tf_op jit(solution)/shard_map/reduce_scatter | solution.py:83
  628.1 39.8 %psum.30 = f32[32,64]{0,1:T(8,128)S(1)} all-reduce(f32[32,64]{0,1:T(8,128)S(1)} %convolution_bitcast_fusion.2), channel_id=1, replica_groups=mesh['user'=8,'item'=4] {'user','item'}, use_global_device_ids=true, to_apply=%region_9.10 | all-reduce | flops 2048 | bytes 16384 | tf_op jit(solution)/shard_map/psum | solution.py:89
  669.2 39.6 %psum.31 = f32[64]{0:T(128)S(1)} all-reduce(f32[64]{0:T(128)S(1)} %get-tuple-element.277), channel_id=1, replica_groups=mesh['user'=8,'item'=4] {'user','item'}, use_global_device_ids=true, to_apply=%region_11.12 | all-reduce | flops 64 | bytes 512 | tf_op jit(solution)/shard_map/psum | solution.py:91
  (186 shorter events, 123.5 us)
Async XLA Ops:
  7.2 0.8 copy-start
  7.2 86.0 %all-gather.2.cloned.1.call-start = ((), (), s32[]{:S(2)}) async-start(), calls=%async_computation.1 | async-start | bytes 1179648 | tf_op jit(solution)/shard_map/all_gather | solution.py:43
  53.0 573.9 %reduce-scatter.2.cloned.1.call-start = ((), (), s32[]{:S(2)}) async-start(), calls=%async_computation.2 | async-start | bytes 2359296 | tf_op jit(solution)/shard_map/reduce_scatter | solution.py:83
  102.3 0.7 copy-start.2
  102.3 0.7 copy-start.3
  237.6 1.8 copy-start.1
Sparse Core Ops, SparseCore 0:
  53.1 40.0 all-gather.1
  304.4 322.5 reduce-scatter.1
where the time goes:
time: 721 us; the launch traced here: 716 us
  waiting for transfers between devices  361 us (50%)
  blocking collectives  176 us (24%)
  other arithmetic  69.8 us (10%)
  local copies, waits for them, and re-layouts  66.5 us (9%)
  matrix products  27.5 us (4%)
  between operations  14.8 us (2%)
    reduce_scatter x1, waiting for transfers between devices, on_device(): lax.psum_scatter(wpart.reshape(nblocks * tile, width), 'user', scatter_di...  321 us
    psum x1, blocking collectives, on_device(): usum = lax.psum(upart.reshape(RB * tile, width), 'item')  54.7 us
    psum x1, blocking collectives, start_reduce(): proj = lax.psum(proj, ('user', 'item'))  42 us
    psum x1, blocking collectives, on_device(): proj2 = lax.psum(proj_back, ('user', 'item'))  39.8 us
    psum x1, blocking collectives, on_device(): colsq = lax.psum(jnp.sum(rest * rest, axis=0), ('user', 'item'))  39.6 us
    all_gather x1, waiting for transfers between devices, on_device(): vslab = lax.all_gather(deflated, 'user', axis=0, tiled=True)  39.5 us
    gather x11, local copies, waits for them, and re-layouts, backward_step(): ublocks[grows]  24.6 us
    gather x11, local copies, waits for them, and re-layouts, forward_step(): vblocks[gcols]  24.6 us
  transfers between devices with their start and end apart: 2, of which 2 were waited for; matrix products, arithmetic and copies ran while one was open for 0% of the time, Pallas kernels for 0%

commit v1 on v0

v1 whole, which is shorter than its diff:
```python
import jax
import jax.numpy as jnp
from jax import lax
from jax.experimental import pallas as pl
from jax.experimental.pallas import tpu as pltpu
from jax.sharding import PartitionSpec as P

TILE = 128
RB = 64
GROUP = 16
SCALE = 1.0 / 1024.0
HIGH = lax.Precision.HIGHEST
NT = (((1,), (1,)), ((), ()))
NN = (((1,), (0,)), ((), ()))


def forward_kernel(rows, cols, seeds, count, v_ref, tiles_ref, u_ref, acc):
    g = pl.program_id(0)
    blocks = u_ref.shape[0]

    @pl.when(g == 0)
    def _():
        acc[...] = jnp.zeros_like(acc)

    @pl.when(g * GROUP < count[0, 0])
    def _():
        a = lax.broadcasted_iota(jnp.int32, (TILE, TILE), 0)
        b = lax.broadcasted_iota(jnp.int32, (TILE, TILE), 1)
        base = (a * TILE + b) * 40503
        for j in range(GROUP):
            s = g * GROUP + j
            h = base + seeds[0, s] * 9973
            h = h ^ (h >> 13)
            h = h * 1597334677
            h = h ^ (h >> 16)
            tile = (((h >> 8) & 255) - 128).astype(jnp.float32).astype(jnp.bfloat16)
            tiles_ref[j] = tile
            row = jnp.where(s < count[0, 0], rows[0, s], blocks)
            acc[row] += lax.dot_general(
                v_ref[cols[0, s]], tile, NT, preferred_element_type=jnp.float32
            )

    @pl.when(g == pl.num_programs(0) - 1)
    def _():
        u_ref[...] = (acc[:blocks] * SCALE).astype(u_ref.dtype)


def backward_kernel(rows, cols, count, u_ref, tiles_ref, w_ref, acc):
    g = pl.program_id(0)
    blocks = w_ref.shape[0]

    @pl.when(g == 0)
    def _():
        acc[...] = jnp.zeros_like(acc)

    @pl.when(g * GROUP < count[0, 0])
    def _():
        for j in range(GROUP):
            s = g * GROUP + j
            col = jnp.where(s < count[0, 0], cols[0, s], blocks)
            acc[col] += lax.dot_general(
                u_ref[rows[0, s]], tiles_ref[j], NN, preferred_element_type=jnp.float32
            )

    @pl.when(g == pl.num_programs(0) - 1)
    def _():
        w_ref[...] = (acc[:blocks] * SCALE).astype(w_ref.dtype)


def tile_spec(count_at):
    def index(g, *refs):
        last = lax.div(refs[count_at][0, 0] + (GROUP - 1), GROUP) - 1
        return (jnp.minimum(g, last), 0, 0)

    return pl.BlockSpec((GROUP, TILE, TILE), index)


def whole_spec(shape):
    return pl.BlockSpec(shape, lambda g, *refs: (0,) * len(shape))


def forward(rows, cols, seeds, count, vblocks, dtype):
    nblocks, width, tile = vblocks.shape
    slots = rows.shape[1]
    out = (RB, width, tile)
    return pl.pallas_call(
        forward_kernel,
        name="forward",
        out_shape=(
            jax.ShapeDtypeStruct((slots, tile, tile), jnp.bfloat16),
            jax.ShapeDtypeStruct(out, dtype),
        ),
        grid_spec=pltpu.PrefetchScalarGridSpec(
            num_scalar_prefetch=4,
            grid=(slots // GROUP,),
            in_specs=[whole_spec(vblocks.shape)],
            out_specs=[tile_spec(3), whole_spec(out)],
            scratch_shapes=[pltpu.VMEM((RB + 1, width, tile), jnp.float32)],
        ),
        compiler_params=pltpu.CompilerParams(vmem_limit_bytes=32 << 20),
    )(rows, cols, seeds, count, vblocks)


def backward(rows, cols, count, ublocks, tiles, nblocks, dtype):
    width, tile = ublocks.shape[1:]
    slots = rows.shape[1]
    out = (nblocks, width, tile)
    return pl.pallas_call(
        backward_kernel,
        name="backward",
        out_shape=jax.ShapeDtypeStruct(out, dtype),
        grid_spec=pltpu.PrefetchScalarGridSpec(
            num_scalar_prefetch=3,
            grid=(slots // GROUP,),
            in_specs=[whole_spec(ublocks.shape), tile_spec(2)],
            out_specs=whole_spec(out),
            scratch_shapes=[pltpu.VMEM((nblocks + 1, width, tile), jnp.float32)],
        ),
        compiler_params=pltpu.CompilerParams(vmem_limit_bytes=32 << 20),
    )(rows, cols, count, ublocks, tiles)


def blocks_of(x):
    return x.reshape(-1, TILE, x.shape[1]).transpose(0, 2, 1)


def rows_of(blocks):
    return blocks.transpose(0, 2, 1).reshape(-1, blocks.shape[1])


def on_device(v_start, locked, tile_rows, tile_cols, tile_seeds, tile_count):
    both = ("user", "item")
    lockf = locked.astype(jnp.float32)
    nlock = locked.shape[1]
    n_user, n_item = lax.axis_size("user"), lax.axis_size("item")
    slab = v_start.shape[0] * n_user
    stats = jnp.dot(
        locked.T, jnp.concatenate([v_start, locked], axis=1), preferred_element_type=jnp.float32
    )
    stats = lax.psum(stats, both)
    proj, gram = stats[:, :-nlock], stats[:, -nlock:]
    deflated = (v_start.astype(jnp.float32) - jnp.dot(lockf, proj, precision=HIGH)).astype(
        jnp.bfloat16
    )
    vslab = lax.all_gather(deflated, "user", axis=0, tiled=True)
    tiles, upart = forward(
        tile_rows, tile_cols, tile_seeds, tile_count, blocks_of(vslab), jnp.float32
    )
    ublocks = lax.psum(upart, "item").astype(jnp.bfloat16)
    per = RB // n_item
    u_factor = rows_of(lax.dynamic_slice_in_dim(ublocks, lax.axis_index("item") * per, per, 0))
    wpart = backward(
        tile_rows, tile_cols, tile_count, ublocks, tiles, slab // TILE, jnp.float32
    )
    back = lax.psum_scatter(rows_of(wpart), "user", scatter_dimension=0, tiled=True)
    sums = jnp.concatenate(
        [jnp.dot(lockf.T, back, precision=HIGH), jnp.sum(back * back, axis=0)[None]], axis=0
    )
    sums = lax.psum(sums, both)
    proj2, backsq = sums[:-1], sums[-1]
    rest = back - jnp.dot(lockf, proj2, precision=HIGH)
    crossed = jnp.dot(gram, proj2, precision=HIGH) - 2.0 * proj2
    colsq = jnp.maximum(backsq + jnp.sum(proj2 * crossed, axis=0), 0.0)
    v_next = rest / jnp.sqrt(colsq / (slab * n_item) + 1e-06)
    return (u_factor, v_next)


def solution(mesh):
    spec = P(("user", "item"), None)
    return jax.shard_map(
        on_device, mesh=mesh, in_specs=(spec,) * 6, out_specs=(spec, spec), check_vma=False
    )
```

time: 721 us -> 295 us (0.41)
  waiting for transfers between devices: 361 us -> 119 us
  other arithmetic: 69.8 us -> 1.09 us
  blocking collectives: 176 us -> 123 us
  local copies, waits for them, and re-layouts: 66.5 us -> 15.2 us
  matrix products: 27.5 us -> 6.41 us
  Pallas kernels: 0 us -> 14.4 us
    reduce_scatter x1, waiting for transfers between devices: 321 us -> 79.5 us  [on_device(): lax.psum_scatter(rows_of(wpart), 'user', scatter_dimension=0, tiled=True)]
    psum x4 -> x3, blocking collectives: 176 us -> 123 us  [the longest x1 42.1 us: on_device(): stats = lax.psum(stats, both)]
    gather x22 -> x0, local copies, waits for them, and re-layouts: 49.2 us -> none  [the longest x11 24.6 us: backward_step(): ublocks[grows]]
    scatter-add x22 -> x0, other arithmetic: 29.3 us -> none  [the longest x11 14.7 us: forward_step(): return (buffer, upart.at[grows].add(prod))]
    dot_general x26 -> x5, matrix products: 27.5 us -> 6.41 us  [the longest x1 1.98 us: on_device(): rest = back - jnp.dot(lockf, proj2, precision=HIGH)]
    pallas_call x0 -> x2, Pallas kernels: none -> 14.4 us  [the longest x1 9.03 us: forward(): pl.pallas_call(forward_kernel, name='forward', out_shape=(jax.ShapeDtypeS...]
    lt x22 -> x0, other arithmetic: 14.3 us -> none  [the longest x11 7.18 us: backward_step(): prod = jnp.where((start + offsets < count)[:, None, None], prod, 0.0)]
    dynamic_update_slice x11 -> x0, other arithmetic: 14.2 us -> none  [forward_step(): buffer = lax.dynamic_update_slice_in_dim(buffer, tiles, start, 0)]
where the time goes in v1:
time: 295 us; the launch traced here: 294 us
  blocking collectives  123 us (42%)
  waiting for transfers between devices  119 us (40%)
  local copies, waits for them, and re-layouts  15.2 us (5%)
  between operations  14.8 us (5%)
  Pallas kernels  14.4 us (5%)
  matrix products  6.41 us (2%)
    reduce_scatter x1, waiting for transfers between devices, on_device(): lax.psum_scatter(rows_of(wpart), 'user', scatter_dimension=0, tiled=True)  79.5 us
    psum x1, blocking collectives, on_device(): stats = lax.psum(stats, both)  42.1 us
    psum x1, blocking collectives, on_device(): ublocks = lax.psum(upart, 'item').astype(jnp.bfloat16)  41.4 us
    psum x1, blocking collectives, on_device(): sums = lax.psum(sums, both)  39.8 us
    all_gather x1, waiting for transfers between devices, on_device(): vslab = lax.all_gather(deflated, 'user', axis=0, tiled=True)  39.5 us
    unnamed x12, local copies, waits for them, and re-layouts  11.5 us
    pallas_call x1, Pallas kernels, forward(): pl.pallas_call(forward_kernel, name='forward', out_shape=(jax.ShapeDtypeS...  9.03 us
  transfers between devices with their start and end apart: 2, of which 2 were waited for; matrix products, arithmetic and copies ran while one was open for 0% of the time, Pallas kernels for 0%

profile of v1, /device:TPU:0, one launch (start us, length us, event | category | flops | bytes accessed | tf_op | source)
XLA Modules:
  0.0 294.4 jit_solution(7067432891547530108)
XLA Ops:
  7.2 0.0 copy-start.4
  7.2 0.0 all-gather.2.cloned.1.call-start
  7.2 1.1 convolution_bitcast_fusion.3
  8.3 42.1 %psum.21 = f32[32,96]{1,0:T(8,128)S(1)} all-reduce(f32[32,96]{1,0:T(8,128)S(1)} %convolution_bitcast_fusion.3), channel_id=1, replica_groups=mesh['user'=8,'item'=4] {'user','item'}, use_global_device_ids=true, to_apply=%region_0.0 | all-reduce | flops 3072 | bytes 24576 | tf_op jit(solution)/shard_map/psum | solution.py:140
  50.4 1.9 fusion.3
  52.3 0.0 all-gather.2.cloned.1.call-update
  52.3 0.0 reduce-scatter.2.cloned.1.call-start
  53.0 39.5 %all-gather.2.cloned.1.call-done = bf16[8192,64]{0,1:T(8,128)(2,1)} async-done(((bf16[1024,64]{0,1:T(8,128)(2,1)}), bf16[8192,64]{0,1:T(8,128)(2,1)}) %all-gather.2.cloned.1.call-update) | async-done | bytes 1048592 | tf_op jit(solution)/shard_map/all_gather | solution.py:145
  92.5 1.5 bitcast_bitcast_fusion.v_ref
  94.1 9.0 %forward.1 = (bf16[512,128,128]{2,1,0:T(8,128)(2,1)S(1)}, f32[64,64,128]{2,1,0:T(8,128)S(1)}) custom-call(s32[1,512]{1,0:T(1,128)S(1)} %copy-done.2, s32[1,512]{1,0:T(1,128)S(1)} %copy-done.3, s32[1,512]{1,0:T(1,128)S(1)} %copy-done.4, s32[1,1]{1,0:T(1,128)S(6)} %copy.19.count, bf16[64,64,128]{2,1,0:T(8,128)(2,1)S(1)} %bitcast_bitcast_fusion.v_ref), custom_call_target="tpu_custom_call" | custom-call | tf_op jit(solution)/shard_map/forward/pallas_call | solution.py:86
  103.1 5.7 %copy-done = bf16[512,128,128]{2,1,0:T(8,128)(2,1)} copy-done((bf16[512,128,128]{2,1,0:T(8,128)(2,1)}, bf16[512,128,128]{2,1,0:T(8,128)(2,1)S(1)}, u32[]{:S(2)}) %copy-start) | copy-done | bytes 16777240
  108.8 41.4 %all-reduce.1.u_ref = bf16[64,64,128]{2,1,0:T(8,128)(2,1)S(1)} all-reduce(f32[64,64,128]{2,1,0:T(8,128)S(1)} %get-tuple-element.4), channel_id=1, replica_groups=mesh['user'=8,'item'=4] {'item'}, use_global_device_ids=true, to_apply=%region_1.0 | all-reduce | flops 524288 | bytes 3145728 | tf_op jit(solution)/shard_map/psum | solution.py:149
  150.3 5.8 %copy-done.1 = bf16[512,128,128]{2,1,0:T(8,128)(2,1)S(1)} copy-done((bf16[512,128,128]{2,1,0:T(8,128)(2,1)S(1)}, bf16[512,128,128]{2,1,0:T(8,128)(2,1)}, u32[]{:S(2)}) %copy-start.1) | copy-done | bytes 16777240
  156.0 5.4 %backward.1 = f32[64,64,128]{2,1,0:T(8,128)S(1)} custom-call(s32[1,512]{1,0:T(1,128)S(1)} %copy-done.2, s32[1,512]{1,0:T(1,128)S(1)} %copy-done.3, s32[1,1]{1,0:T(1,128)S(6)} %copy.19.count, bf16[64,64,128]{2,1,0:T(8,128)(2,1)S(1)} %all-reduce.1.u_ref, bf16[512,128,128]{2,1,0:T(8,128)(2,1)S(1)} %copy-done.1), custom_call_target="tpu_custom_call" | custom-call | tf_op jit(solution)/shard_map/backward/pallas_call | solution.py:108
  161.4 1.5 copy_bitcast_fusion
  162.9 0.0 reduce-scatter.2.cloned.1.call-update
  163.0 0.7 copy_bitcast_fusion.1
  163.7 79.5 %reduce-scatter.2.cloned.1.call-done = f32[1024,64]{0,1:T(8,128)} async-done(((f32[8192,64]{0,1:T(8,128)}), f32[1024,64]{0,1:T(8,128)}) %reduce-scatter.2.cloned.1.call-update) | async-done | bytes 262160 | tf_op jit(solution)/shard_map/reduce_scatter | solution.py:155
  243.2 0.0 copy-done.5
  243.2 1.2 convolution_bitcast_fusion.2
  244.4 1.1 multiply_reduce_fusion
  245.5 39.8 %psum.23 = f32[33,64]{1,0:T(8,128)S(1)} all-reduce(f32[33,64]{1,0:T(8,128)S(1)} %pad_maximum_fusion), channel_id=1, replica_groups=mesh['user'=8,'item'=4] {'user','item'}, use_global_device_ids=true, to_apply=%region_4.0 | all-reduce | flops 2112 | bytes 16896 | tf_op jit(solution)/shard_map/psum | solution.py:159
  285.3 0.2 fusion.5
  285.6 2.0 fusion.1
  (10 shorter events, 0.0 us)
Async XLA Ops:
  7.2 86.9 %copy-start.4 = (s32[1,512]{1,0:T(1,128)S(1)}, s32[1,512]{1,0:T(1,128)}, u32[]{:S(2)}) copy-start(s32[1,512]{1,0:T(1,128)} %seeds.1) | copy-start | bytes 6148
  7.2 86.9 %copy-start.2 = (s32[1,512]{1,0:T(1,128)S(1)}, s32[1,512]{1,0:T(1,128)}, u32[]{:S(2)}) copy-start(s32[1,512]{1,0:T(1,128)} %rows.3) | copy-start | bytes 6148
  7.2 86.9 %copy-start.3 = (s32[1,512]{1,0:T(1,128)S(1)}, s32[1,512]{1,0:T(1,128)}, u32[]{:S(2)}) copy-start(s32[1,512]{1,0:T(1,128)} %cols.3) | copy-start | bytes 6148
  7.2 85.3 %all-gather.2.cloned.1.call-start = ((), (), s32[]{:S(2)}) async-start(), calls=%async_computation.1 | async-start | bytes 1179648 | tf_op jit(solution)/shard_map/all_gather | solution.py:145
  52.3 190.8 %reduce-scatter.2.cloned.1.call-start = ((), (), s32[]{:S(2)}) async-start(), calls=%async_computation.2 | async-start | bytes 2359296 | tf_op jit(solution)/shard_map/reduce_scatter | solution.py:155
  103.1 5.7 %copy-start = (bf16[512,128,128]{2,1,0:T(8,128)(2,1)}, bf16[512,128,128]{2,1,0:T(8,128)(2,1)S(1)}, u32[]{:S(2)}) copy-start(bf16[512,128,128]{2,1,0:T(8,128)(2,1)S(1)} %get-tuple-element.5.tiles_ref) | copy-start | bytes 50331652
  150.3 5.8 %copy-start.1 = (bf16[512,128,128]{2,1,0:T(8,128)(2,1)S(1)}, bf16[512,128,128]{2,1,0:T(8,128)(2,1)}, u32[]{:S(2)}) copy-start(bf16[512,128,128]{2,1,0:T(8,128)(2,1)} %copy-done) | copy-start | bytes 50331652
  162.9 80.2 %copy-start.5 = (bf16[1024,32]{0,1:T(8,128)(2,1)S(1)}, bf16[1024,32]{0,1:T(8,128)(2,1)}, u32[]{:S(2)}) copy-start(bf16[1024,32]{0,1:T(8,128)(2,1)} %param.7) | copy-start | bytes 196612
Sparse Core Ops, SparseCore 0:
  52.5 40.0 all-gather.1
  163.1 80.0 reduce-scatter.1

commit v2 on v1

--- a/solution.py
+++ b/solution.py
@@ -1,3 +1,5 @@
+import functools
+
 import jax
 import jax.numpy as jnp
 from jax import lax
@@ -128,7 +130,243 @@
     return blocks.transpose(0, 2, 1).reshape(-1, blocks.shape[1])
 
 
+MESH = pl.DeviceIdType.MESH
+CHUNKS = 4
+
+
+def peers(axis):
+    n, me = lax.axis_size(axis), lax.axis_index(axis)
+    return [{axis: lax.rem(me + o, n)} for o in range(1, n)]
+
+
+def meet(devices):
+    barrier = pltpu.get_barrier_semaphore()
+    for device in devices:
+        pl.semaphore_signal(barrier, inc=1, device_id=device, device_id_type=MESH)
+    pl.semaphore_wait(barrier, len(devices))
+
+
+def remote(src, dst, send, recv, device):
+    return pltpu.make_async_remote_copy(
+        src_ref=src, dst_ref=dst, send_sem=send, recv_sem=recv, device_id=device,
+        device_id_type=MESH,
+    )
+
+
+def sum_over(axis, value, slots, send, recv):
+    n, me = lax.axis_size(axis), lax.axis_index(axis)
+    slots[me] = value
+    copies = [
+        remote(slots.at[me], slots.at[me], send.at[o], recv.at[o], device)
+        for o, device in enumerate(peers(axis))
+    ]
+    for copy in copies:
+        copy.start()
+    for copy in copies:
+        copy.wait()
+    total = slots[0]
+    for i in range(1, n):
+        total = total + slots[i]
+    return total
+
+
+def gather_kernel(cat_ref, v_ref, stats_ref, slots_i, slots_u, si, ri, su, ru, sg, rg):
+    nlock = stats_ref.shape[0]
+    width = v_ref.shape[1]
+    meet(peers("item") + peers("user"))
+    lock = cat_ref[:nlock]
+    stats = lax.dot_general(lock, cat_ref[...], NT, preferred_element_type=jnp.float32)
+    stats = sum_over("item", stats, slots_i, si, ri)
+    stats = sum_over("user", stats, slots_u, su, ru)
+    stats_ref[...] = stats
+    projt = stats.T[nlock : nlock + width]
+    own = cat_ref.shape[1] // TILE
+    first = lax.axis_index("user") * own
+    for j in range(own):
+        at = slice(j * TILE, (j + 1) * TILE)
+        v = cat_ref[nlock : nlock + width, at].astype(jnp.float32)
+        part = jnp.dot(projt, cat_ref[:nlock, at].astype(jnp.float32), precision=HIGH)
+        v_ref[first + j] = (v - part).astype(v_ref.dtype)
+    mine = v_ref.at[pl.ds(first, own)]
+    copies = [
+        remote(mine, mine, sg.at[o], rg.at[o], device)
+        for o, device in enumerate(peers("user"))
+    ]
+    for copy in copies:
+        copy.start()
+    for copy in copies:
+        copy.wait()
+
+
+def user_sum_kernel(part_ref, u_ref, near, pair, far, sem):
+    me = lax.axis_index("item")
+    side = lax.rem(me, 2)
+    sibling = {"item": me + 1 - 2 * side}
+    across = {"item": lax.rem(me + 2, 4)}
+    half = part_ref.shape[0] // 2
+    size = half // CHUNKS
+    meet([sibling, across])
+
+    def copies(step, src, src_at, dst, dst_at, device):
+        return [
+            remote(
+                src.at[pl.ds(src_at + k * size, size)],
+                dst.at[pl.ds(dst_at + k * size, size)],
+                sem.at[2 * step, k],
+                sem.at[2 * step + 1, k],
+                device,
+            )
+            for k in range(CHUNKS)
+        ]
+
+    give = copies(0, part_ref, (1 - side) * half, near, 0, sibling)
+    swap = copies(1, pair, 0, far, 0, across)
+    back = copies(2, u_ref, side * half, u_ref, side * half, sibling)
+    for copy in give:
+        copy.start()
+    for k in range(CHUNKS):
+        give[k].wait_recv()
+        at = pl.ds(k * size, size)
+        own = part_ref[pl.ds(side * half + k * size, size)].astype(jnp.float32)
+        pair[at] = (own + near[at].astype(jnp.float32)).astype(pair.dtype)
+        swap[k].start()
+    for k in range(CHUNKS):
+        swap[k].wait_recv()
+        at = pl.ds(k * size, size)
+        total = pair[at].astype(jnp.float32) + far[at].astype(jnp.float32)
+        u_ref[pl.ds(side * half + k * size, size)] = total.astype(u_ref.dtype)
+        back[k].start()
+    for k in range(CHUNKS):
+        give[k].wait_send()
+        swap[k].wait_send()
+        back[k].wait()
+
+
+def finish_kernel(
+    items, part_ref, lock_ref, stats_ref, v_ref, land, slots_i, slots_u, s, r, si, ri, su, ru
+):
+    nlock = stats_ref.shape[0]
+    own, width, tile = land.shape[1:]
+    n, me = lax.axis_size("user"), lax.axis_index("user")
+    meet(peers("item") + peers("user"))
+    copies = [
+        remote(
+            part_ref.at[pl.ds(device["user"] * own, own)], land.at[me], s.at[o], r.at[o], device
+        )
+        for o, device in enumerate(peers("user"))
+    ]
+    for copy in copies:
+        copy.start()
+    land[me] = part_ref[pl.ds(me * own, own)]
+    for copy in copies:
+        copy.wait()
+    back, sums = [], jnp.zeros((width, tile), jnp.float32)
+    square = jnp.zeros((width, tile), jnp.float32)
+    for j in range(own):
+        b = land[0, j].astype(jnp.float32)
+        for i in range(1, n):
+            b = b + land[i, j].astype(jnp.float32)
+        back.append(b)
+        square = square + b * b
+        lock = lock_ref[:, j * tile : (j + 1) * tile].astype(jnp.float32)
+        sums = sums + lax.dot_general(
+            b, lock, NT, precision=HIGH, preferred_element_type=jnp.float32
+        )
+    lane = lax.broadcasted_iota(jnp.int32, (width, tile), 1)
+    sums = jnp.where(lane == nlock, jnp.sum(square, axis=1, keepdims=True), sums)
+    sums = sum_over("item", sums, slots_i, si, ri)
+    sums = sum_over("user", sums, slots_u, su, ru)
+    proj2, backsq = sums[:, :nlock], sums[:, nlock : nlock + 1]
+    gram = stats_ref[:, :nlock]
+    crossed = jnp.dot(proj2, gram, precision=HIGH) - 2.0 * proj2
+    colsq = backsq + jnp.sum(proj2 * crossed, axis=1, keepdims=True)
+    scale = 1.0 / jnp.sqrt(jnp.maximum(colsq, 0.0) / items + 1e-06)
+    for j in range(own):
+        lock = lock_ref[:nlock, j * tile : (j + 1) * tile].astype(jnp.float32)
+        rest = back[j] - jnp.dot(proj2, lock, precision=HIGH)
+        v_ref[j * tile : (j + 1) * tile, :] = (rest * scale).T
+
+
+def comm_call(kernel, name, key, out_shape, scratch, *args):
+    vmem = pl.BlockSpec(memory_space=pltpu.VMEM)
+    return pl.pallas_call(
+        kernel,
+        name=name,
+        out_shape=out_shape,
+        in_specs=[vmem] * len(args),
+        out_specs=jax.tree.map(lambda _: vmem, out_shape),
+        scratch_shapes=scratch,
+        compiler_params=pltpu.CompilerParams(
+            collective_id=key, has_side_effects=True, vmem_limit_bytes=32 << 20
+        ),
+    )(*args)
+
+
+def sems(*shape):
+    return pltpu.SemaphoreType.DMA(shape)
+
+
+def remote_plan(v_start, locked, tile_rows, tile_cols, tile_seeds, tile_count):
+    n_user, n_item = lax.axis_size("user"), lax.axis_size("item")
+    shard, width = v_start.shape
+    nlock = locked.shape[1]
+    nblocks = shard * n_user // TILE
+    pad = jnp.zeros((shard, TILE - nlock - width), v_start.dtype)
+    cat = jnp.concatenate([locked, v_start, pad], axis=1).T
+    slab = (nblocks, width, TILE)
+    pair = [sems(n_item - 1)] * 2 + [sems(n_user - 1)] * 2
+    vblocks, stats = comm_call(
+        gather_kernel,
+        "gather",
+        0,
+        (
+            jax.ShapeDtypeStruct(slab, jnp.bfloat16),
+            jax.ShapeDtypeStruct((nlock, TILE), jnp.float32),
+        ),
+        [
+            pltpu.VMEM((n_item, nlock, TILE), jnp.float32),
+            pltpu.VMEM((n_user, nlock, TILE), jnp.float32),
+        ]
+        + pair
+        + [sems(n_user - 1)] * 2,
+        cat,
+    )
+    tiles, upart = forward(tile_rows, tile_cols, tile_seeds, tile_count, vblocks, jnp.bfloat16)
+    half = pltpu.VMEM((RB // 2, width, TILE), jnp.bfloat16)
+    ublocks = comm_call(
+        user_sum_kernel,
+        "user_sum",
+        1,
+        jax.ShapeDtypeStruct((RB, width, TILE), jnp.bfloat16),
+        [half, half, half, sems(6, CHUNKS)],
+        upart,
+    )
+    wpart = backward(tile_rows, tile_cols, tile_count, ublocks, tiles, nblocks, jnp.bfloat16)
+    per = RB // n_item
+    u_factor = rows_of(lax.dynamic_slice_in_dim(ublocks, lax.axis_index("item") * per, per, 0))
+    only = jnp.concatenate([locked, jnp.zeros((shard, TILE - nlock), locked.dtype)], axis=1).T
+    v_next = comm_call(
+        functools.partial(finish_kernel, float(shard * n_user * n_item)),
+        "finish",
+        2,
+        jax.ShapeDtypeStruct((shard, width), jnp.float32),
+        [
+            pltpu.VMEM((n_user, nblocks // n_user, width, TILE), jnp.bfloat16),
+            pltpu.VMEM((n_item, width, TILE), jnp.float32),
+            pltpu.VMEM((n_user, width, TILE), jnp.float32),
+        ]
+        + [sems(n_user - 1)] * 2
+        + pair,
+        wpart,
+        only,
+        stats,
+    )
+    return (u_factor, v_next)
+
+
 def on_device(v_start, locked, tile_rows, tile_cols, tile_seeds, tile_count):
+    if v_start.shape[0] % TILE == 0 and lax.axis_size("item") == 4:
+        return remote_plan(v_start, locked, tile_rows, tile_cols, tile_seeds, tile_count)
     both = ("user", "item")
     lockf = locked.astype(jnp.float32)
     nlock = locked.shape[1]

time: 295 us -> 130 us (0.44)
  blocking collectives: 123 us -> 0 us
  waiting for transfers between devices: 119 us -> 0 us
  Pallas kernels: 14.4 us -> 110 us
  between operations: 14.8 us -> 1.36 us
  matrix products: 6.41 us -> 0 us
    psum x3 -> x0, blocking collectives: 123 us -> none  [the longest x1 42.1 us: on_device(): stats = lax.psum(stats, both)]
    pallas_call x0 -> x3, Pallas kernels: none -> 97.4 us  [comm_call(): pl.pallas_call(kernel, name=name, out_shape=out_shape, in_specs=[vmem] *...]
    reduce_scatter x1 -> x0, waiting for transfers between devices: 79.5 us -> none  [on_device(): lax.psum_scatter(rows_of(wpart), 'user', scatter_dimension=0, tiled=True)]
    all_gather x1 -> x0, waiting for transfers between devices: 39.5 us -> none  [on_device(): vslab = lax.all_gather(deflated, 'user', axis=0, tiled=True)]
    dot_general x5 -> x0, matrix products: 6.41 us -> none  [the longest x1 1.98 us: on_device(): rest = back - jnp.dot(lockf, proj2, precision=HIGH)]
    unnamed x12 -> x15, local copies, waits for them, and re-layouts: 11.5 us -> 15.8 us
  transfers between devices with their start and end apart: 2 -> 0, of which waited for: 2 -> 0; matrix products, arithmetic and copies ran while one was open for 0% -> 0% of each run, Pallas kernels for 0% -> 0%
where the time goes in v2:
time: 130 us; the launch traced here: 129 us
  Pallas kernels  110 us (85%)
  local copies, waits for them, and re-layouts  16.6 us (13%)
  between operations  1.36 us (1%)
    pallas_call x3, Pallas kernels, comm_call(): pl.pallas_call(kernel, name=name, out_shape=out_shape, in_specs=[vmem] *...  97.4 us
    unnamed x15, local copies, waits for them, and re-layouts  15.8 us
    pallas_call x1, Pallas kernels, forward(): pl.pallas_call(forward_kernel, name='forward', out_shape=(jax.ShapeDtypeS...  7.84 us
    pallas_call x1, Pallas kernels, backward(): pl.pallas_call(backward_kernel, name='backward', out_shape=jax.ShapeDtype...  4.85 us

profile of v2, /device:TPU:0, one launch (start us, length us, event | category | flops | bytes accessed | tf_op | source)
XLA Modules:
  0.0 129.1 jit_solution(1583957967787775075)
XLA Ops:
  0.6 0.1 pad.3.clone
  0.7 1.1 pad_bitcast_fusion
  1.8 32.6 %gather.1 = (bf16[64,64,128]{2,1,0:T(8,128)(2,1)S(1)}, f32[32,128]{1,0:T(8,128)S(1)}) custom-call(bf16[128,1024]{1,0:T(8,128)(2,1)S(1)} %get-tuple-element.15.cat_ref), custom_call_target="tpu_custom_call" | custom-call | tf_op jit(solution)/shard_map/gather/pallas_call | solution.py:292
  35.0 0.0 copy-start.2
  35.0 0.7 copy-done.2
  35.7 0.0 copy-start.4
  35.7 0.7 copy-done.4
  36.4 0.0 copy-start.6
  36.4 0.7 copy-done.6
  37.1 7.8 %forward.1 = (bf16[512,128,128]{2,1,0:T(8,128)(2,1)S(1)}, bf16[64,64,128]{2,1,0:T(8,128)(2,1)S(1)}) custom-call(s32[1,512]{1,0:T(1,128)S(1)} %copy-done.2, s32[1,512]{1,0:T(1,128)S(1)} %copy-done.4, s32[1,512]{1,0:T(1,128)S(1)} %copy-done.6, s32[1,1]{1,0:T(1,128)S(6)} %copy.13.count, bf16[64,64,128]{2,1,0:T(8,128)(2,1)S(1)} %get-tuple-element.6.v_ref), custom_call_target="tpu_custom_call" | custom-call | tf_op jit(solution)/shard_map/forward/pallas_call | solution.py:88
  44.9 0.0 copy-start
  44.9 5.7 %copy-done = bf16[512,128,128]{2,1,0:T(8,128)(2,1)} copy-done((bf16[512,128,128]{2,1,0:T(8,128)(2,1)}, bf16[512,128,128]{2,1,0:T(8,128)(2,1)S(1)}, u32[]{:S(2)}) %copy-start) | copy-done | bytes 16777240
  50.6 16.7 %user_sum.1.u_ref = bf16[64,64,128]{2,1,0:T(8,128)(2,1)S(1)} custom-call(bf16[64,64,128]{2,1,0:T(8,128)(2,1)S(1)} %get-tuple-element.7.part_ref), custom_call_target="tpu_custom_call" | custom-call | tf_op jit(solution)/shard_map/user_sum/pallas_call | solution.py:292
  67.4 0.0 copy-start.1
  67.4 5.8 %copy-done.1 = bf16[512,128,128]{2,1,0:T(8,128)(2,1)S(1)} copy-done((bf16[512,128,128]{2,1,0:T(8,128)(2,1)S(1)}, bf16[512,128,128]{2,1,0:T(8,128)(2,1)}, u32[]{:S(2)}) %copy-start.1) | copy-done | bytes 16777240
  73.1 0.0 copy-start.3
  73.2 0.7 copy-done.3
  73.8 0.0 copy-start.5
  73.8 0.7 copy-done.5
  74.5 4.9 %backward.1.part_ref = bf16[64,64,128]{2,1,0:T(8,128)(2,1)S(1)} custom-call(s32[1,512]{1,0:T(1,128)S(1)} %copy-done.3, s32[1,512]{1,0:T(1,128)S(1)} %copy-done.5, s32[1,1]{1,0:T(1,128)S(6)} %copy.13.count, bf16[64,64,128]{2,1,0:T(8,128)(2,1)S(1)} %user_sum.1.u_ref, bf16[512,128,128]{2,1,0:T(8,128)(2,1)S(1)} %copy-done.1), custom_call_target="tpu_custom_call" | custom-call | tf_op jit(solution)/shard_map/backward/pallas_call | solution.py:110
  79.4 48.1 %finish.1 = f32[1024,64]{1,0:T(8,128)S(1)} custom-call(bf16[64,64,128]{2,1,0:T(8,128)(2,1)S(1)} %backward.1.part_ref, bf16[128,1024]{1,0:T(8,128)(2,1)S(1)} %get-tuple-element.14.lock_ref, f32[32,128]{1,0:T(8,128)S(1)} %get-tuple-element.9.stats_ref), custom_call_target="tpu_custom_call" | custom-call | tf_op jit(solution)/shard_map/finish/pallas_call | solution.py:292
  127.5 0.9 copy.10
  128.4 0.7 copy_bitcast_fusion
  (1 shorter events, 0.0 us)
Async XLA Ops:
  35.0 0.7 copy-start.2
  35.7 0.7 copy-start.4
  36.4 0.7 copy-start.6
  44.9 5.7 %copy-start = (bf16[512,128,128]{2,1,0:T(8,128)(2,1)}, bf16[512,128,128]{2,1,0:T(8,128)(2,1)S(1)}, u32[]{:S(2)}) copy-start(bf16[512,128,128]{2,1,0:T(8,128)(2,1)S(1)} %get-tuple-element.8.tiles_ref) | copy-start | bytes 50331652
  67.4 5.8 %copy-start.1 = (bf16[512,128,128]{2,1,0:T(8,128)(2,1)S(1)}, bf16[512,128,128]{2,1,0:T(8,128)(2,1)}, u32[]{:S(2)}) copy-start(bf16[512,128,128]{2,1,0:T(8,128)(2,1)} %copy-done) | copy-start | bytes 50331652
  73.1 0.7 copy-start.3
  73.8 0.7 copy-start.5
